TPU v7x, 128 devices: a whole 4x4x4 slice. The times are simulated.
128 devices in a mesh: row: 16 (over y_lo, x, core), col: 8 (over z, y_hi).
Axes of the slice: x: 4, y: 4 (y_hi: 2, y_lo: 2; y = y_hi * 2 + y_lo), z: 4, core: 2. Of those that a mesh axis runs over, the one named last changes fastest.
Arguments:
- series: bfloat16 [16384, 2048], P(('row', 'col')), may hold values from -6 to 6
- w_in: bfloat16 [2048, 1024], replicated, may hold values from -0.125 to 0.125
- w_out: bfloat16 [1024, 256], replicated, may hold values from -0.1875 to 0.1875
- factor_a: bfloat16 [16384, 32], P(('row', 'col')), may hold values from -3 to 3
- factor_b: bfloat16 [16384, 32], P(('row', 'col')), may hold values from -3 to 3
- mix_weight: float32 [8], replicated, may hold values from 0.2 to 2
- mix_var: float32 [8], replicated, may hold values from 0.0001 to 0.0006
- mix_mean: float32 [8, 256], replicated, may hold values from -0.0625 to 0.0625
Outputs:
- grad_embed: float32 [16384, 256], P(('row', 'col'))
- grad_in: float32 [2048, 1024], P('row', 'col')
- grad_out: float32 [1024, 256], P(('row', 'col'))
- grad_weight: float32 [8], replicated
- grad_var: float32 [8], replicated
- grad_mean: float32 [8, 256], replicated
All inputs are finite; a program needn't handle non-finite values.
Results may differ from a plain program's by a relative error of at most 0.0067.
Values may be sent and summed in bfloat16 or wider, within the bound.
No kernel may reach another device: no remote copies, remote signals or barrier semaphores. Data moves between devices by JAX's collectives and lax.ppermute only.
A program may use at most 192 MiB of HBM per device.

v0:
```python
import math

import jax
import jax.numpy as jnp
from jax import lax
from jax.sharding import PartitionSpec as P

two_pi = 2.0 * math.pi
two_pi_sq = 2.0 * math.pi * math.pi
highest = lax.Precision.HIGHEST


def tile_terms(row_e, row_f, col_e, col_f, row_cos, row_sin, col_cos, col_sin, mix_weight, mix_var):
    row_ef = row_e.astype(jnp.float32)
    col_ef = col_e.astype(jnp.float32)
    cross = lax.dot_general(
        row_e, col_e, (((1,), (1,)), ((), ())), preferred_element_type=jnp.float32
    )
    dist = jnp.sum(row_ef * row_ef, 1)[:, None] + jnp.sum(col_ef * col_ef, 1)[None, :] - 2.0 * cross
    outer = lax.dot_general(
        row_f, col_f, (((1,), (1,)), ((), ())), preferred_element_type=jnp.float32
    )
    coef = jnp.zeros_like(dist)
    spins = []
    weights = []
    varies = []
    for comp in range(mix_weight.shape[0]):
        rate = -two_pi_sq * mix_var[comp]
        damp = outer * jnp.exp(rate * dist)
        cosine = (
            row_cos[comp][:, None] * col_cos[comp][None, :]
            + row_sin[comp][:, None] * col_sin[comp][None, :]
        )
        even = damp * cosine
        coef = coef + mix_weight[comp] * rate * even
        weights.append(0.5 * jnp.sum(even))
        varies.append(0.5 * mix_weight[comp] * -two_pi_sq * jnp.sum(even * dist))
        with_cos = jnp.sum(damp * col_cos[comp][None, :], 1)
        with_sin = jnp.sum(damp * col_sin[comp][None, :], 1)
        spins.append(
            -two_pi * mix_weight[comp] * (row_sin[comp] * with_cos - row_cos[comp] * with_sin)
        )
    rowsum = jnp.sum(coef, 1)
    pulled = jnp.dot(coef, col_ef, precision=highest)
    return (rowsum, pulled, jnp.stack(spins, 0), jnp.stack(weights), jnp.stack(varies))


def phases(mix_mean, embed_f):
    angle = two_pi * lax.dot_general(mix_mean, embed_f, (((1,), (1,)), ((), ())), precision=highest)
    return (jnp.cos(angle), jnp.sin(angle))


def body(series, w_in, w_out, factor_a, factor_b, mix_weight, mix_var, mix_mean):
    pre = jnp.dot(series, w_in, preferred_element_type=jnp.float32)
    hidden = jax.nn.silu(pre).astype(jnp.bfloat16)
    emb = jnp.dot(hidden, w_out, preferred_element_type=jnp.float32).astype(jnp.bfloat16)
    factors = jnp.concatenate([factor_a, factor_b], 1)
    half = factor_a.shape[1]
    row_e, row_f = (
        lax.all_gather(emb, "col", axis=0, tiled=True),
        lax.all_gather(factors, "col", axis=0, tiled=True),
    )
    row_ef = row_e.astype(jnp.float32)
    row_cos, row_sin = phases(mix_mean, row_ef)
    col_e = lax.all_gather(emb, "row", axis=0, tiled=True)
    col_f = lax.all_gather(factors, "row", axis=0, tiled=True)
    col_swap = jnp.concatenate([col_f[:, half:], col_f[:, :half]], 1)
    col_cos, col_sin = phases(mix_mean, col_e.astype(jnp.float32))
    rowsum, pulled, spin, weights, varies = tile_terms(
        row_e, row_f, col_e, col_swap, row_cos, row_sin, col_cos, col_sin, mix_weight, mix_var
    )
    rowsum, pulled, spin, weights, varies = (rowsum, pulled, spin, weights, varies)
    partial_grad = 2.0 * (rowsum[:, None] * row_ef - pulled) + lax.dot_general(
        spin, mix_mean, (((0,), (0,)), ((), ())), precision=highest
    )
    grad_embed = lax.psum_scatter(partial_grad, "col", scatter_dimension=0, tiled=True)
    means = jnp.dot(spin, row_ef, precision=highest)
    grad_weight, grad_var, grad_mean = lax.psum((weights, varies, means), ("row", "col"))
    emb_cot = grad_embed.astype(jnp.bfloat16)
    back = lax.dot_general(
        emb_cot, w_out, (((1,), (1,)), ((), ())), preferred_element_type=jnp.float32
    )
    sigma = jax.nn.sigmoid(pre)
    d_hidden = (back * sigma * (1.0 + pre * (1.0 - sigma))).astype(jnp.bfloat16)
    contract = (((0,), (0,)), ((), ()))
    part = hidden
    grad_out = lax.psum_scatter(
        lax.dot_general(part, emb_cot, contract, preferred_element_type=jnp.float32),
        ("row", "col"),
        scatter_dimension=0,
        tiled=True,
    )
    part = series
    by_input = lax.psum_scatter(
        lax.dot_general(part, d_hidden, contract, preferred_element_type=jnp.float32),
        "row",
        scatter_dimension=0,
        tiled=True,
    )
    grad_in = lax.psum_scatter(by_input, "col", scatter_dimension=1, tiled=True)
    return (grad_embed, grad_in, grad_out, grad_weight, grad_var, grad_mean)


def solution(mesh):
    placed = (
        P(("row", "col"), None),
        P(),
        P(),
        P(("row", "col"), None),
        P(("row", "col"), None),
        P(),
        P(),
        P(),
    )
    return jax.shard_map(
        body,
        mesh=mesh,
        in_specs=placed,
        out_specs=(
            P(("row", "col"), None),
            P("row", "col"),
            P(("row", "col"), None),
            P(),
            P(),
            P(),
        ),
        check_vma=False,
    )
```

profile of v0, /device:TPU:0, one launch (start us, length us, event | category | flops | bytes accessed | tf_op | source)
XLA Modules:
  0.0 1100.7 jit_solution(10301428092646583290)
XLA Ops:
  7.2 0.0 copy-start
  7.2 0.0 copy-start.4
  7.2 0.0 all-gather.2.cloned.1.call-start
  7.2 1.0 copy-done
  8.2 2.9 fusion.34
  11.1 2.0 convolution_convert_fusion
  13.1 0.0 all-gather.2.cloned.1.call-update
  13.1 0.0 reduce-scatter.5.cloned.1.call-start
  13.2 1.6 fusion.33
  14.8 0.7 constant_dynamic-update-slice_fusion.1
  15.5 1.6 fusion.32
  17.1 0.7 constant_dynamic-update-slice_fusion
  33.1 32.4 %all_gather.12 = bf16[1024,64]{0,1:T(8,128)(2,1)S(1)} all-gather(bf16[128,64]{0,1:T(8,128)(2,1)S(1)} %constant_dynamic-update-slice_fusion), channel_id=1, replica_groups=mesh['row'=16,'col'=8] {'col'}, dimensions={0}, use_global_device_ids=true | all-gather | bytes 147456 | tf_op jit(solution)/shard_map/all_gather | solution.py:61
  65.5 20.4 %all_gather.13 = bf16[2048,64]{0,1:T(8,128)(2,1)S(1)} all-gather(bf16[128,64]{0,1:T(8,128)(2,1)S(1)} %constant_dynamic-update-slice_fusion), channel_id=1, replica_groups=mesh['row'=16,'col'=8] {'row'}, dimensions={0}, use_global_device_ids=true | all-gather | bytes 278528 | tf_op jit(solution)/shard_map/all_gather | solution.py:66
  85.9 36.2 %all_gather.14 = bf16[1024,256]{1,0:T(8,128)(2,1)S(1)} all-gather(bf16[128,256]{1,0:T(8,128)(2,1)} %convolution_convert_fusion), channel_id=1, replica_groups=mesh['row'=16,'col'=8] {'col'}, dimensions={0}, use_global_device_ids=true | all-gather | bytes 589824 | tf_op jit(solution)/shard_map/all_gather | solution.py:60
  122.1 0.2 fusion.11
  122.3 0.6 cosine_bitcast_fusion.1
  123.0 4.5 fusion.15
  127.5 2.2 cosine_bitcast_fusion
  129.7 0.1 fusion.28
  129.8 0.0 slice-start
  129.8 1.7 multiply_reduce_fusion.24
  131.5 0.0 slice-start.1
  131.5 22.0 %multiply_reduce_fusion = (f32[]{:T(128)}, f32[]{:T(128)}, f32[1024]{0:T(1024)S(1)}, f32[1024]{0:T(1024)S(1)}, f32[1024]{0:T(1024)S(1)}, /*index=5*/f32[1024]{0:...) fusion(f32[2048]{0:T(1024)S(1)} %bitcast.150, ...), kind=kOutput, calls=%fused_computation | convolution fusion | flops 1161816064 | bytes 43626532 | tf_op jit(solution)/shard_map/dot_general | solution.py:16
  153.6 13.9 %multiply_reduce_fusion.6 = (f32[]{:T(128)}, f32[]{:T(128)}, f32[1024]{0:T(1024)S(1)}, f32[1024]{0:T(1024)S(1)}, f32[1024]{0:T(1024)S(1)}, /*index=5*/f32[1024]{...) fusion(f32[1024,2048]{1,0:T(8,128)S(1)} %get-tuple-element.139, f32[2048]{0:T(1024)S(1)} %bitcast.118, ...), kind=kLoop, calls=%fused_computation.6 | loop fusion | flops 54521856 | bytes 33619992 | tf_op jit(solution)/shard_map/reduce_sum | solution.py:37
  167.5 21.8 %multiply_reduce_fusion.3 = (f32[]{:T(128)}, f32[]{:T(128)}, f32[1024]{0:T(1024)S(1)}, f32[1024]{0:T(1024)S(1)}, f32[1024]{0:T(1024)S(1)}, /*index=5*/f32[1024]{...) fusion(f32[1024,2048]{1,0:T(8,128)S(1)} %get-tuple-element.139,, ...), kind=kLoop, calls=%fused_computation.3 | loop fusion | flops 81782784 | bytes 42041380 | tf_op jit(solution)/shard_map/reduce_sum | solution.py:37
  189.4 0.1 stack.65
  189.4 25.1 %fusion.26 = (f32[1024]{0:T(1024)S(1)}, f32[1024,2048]{1,0:T(8,128)}) fusion(f32[1024,2048]{1,0:T(8,128)} %get-tuple-element.67, f32[2048]{0:T(1024)S(1)} %bitcast.151, f32[1024]{0:T(1024)S(1)} %bitcast.173, f32[2048]{0:T(1024)S(1)} %bitcast.161, f32[1024]{0:T(1024)S(1)} %bitcast.163, f32[]{:T(128)S(6)} %mul.1029, f32[1024,2048]{1,0:T(8,128)} %get-tuple-element.68, ...), kind=kLoop, calls=%fused_computation.93 | loop fusion | flops 100662272 | bytes 75698208 | tf_op jit(solution)/shard_map/reduce_sum | solution.py:43
  214.6 0.0 copy-start.2
  214.6 6.4 fusion.8
  221.1 2.1 convolution_add_fusion
  223.1 0.0 reduce-scatter.5.cloned.1.call-update
  223.1 0.0 reduce-scatter.7.cloned.1.call-start
  223.2 69.7 %reduce-scatter.5.cloned.1.call-done = f32[128,256]{1,0:T(8,128)} async-done(((f32[1024,256]{1,0:T(8,128)}), f32[128,256]{1,0:T(8,128)}) %reduce-scatter.5.cloned.1.call-update) | async-done | bytes 131088 | tf_op jit(solution)/shard_map/reduce_scatter | solution.py:76
  292.9 5.7 convolution_bitcast_fusion
  298.6 0.0 reduce-scatter.7.cloned.1.call-update
  298.6 0.0 reduce-scatter.9.cloned.1.call-start
  298.7 73.9 %reduce-scatter.7.cloned.1.call-done = f32[128,1024]{0,1:T(8,128)} async-done(((f32[2048,1024]{0,1:T(8,128)}), f32[128,1024]{0,1:T(8,128)}) %reduce-scatter.7.cloned.1.call-update) | async-done | bytes 524304 | tf_op jit(solution)/shard_map/reduce_scatter | solution.py:94
  372.6 0.0 reduce-scatter.9.cloned.1.call-update
  372.6 0.0 reduce-scatter.11.cloned.1.call-start
  372.7 1.4 fusion.20
  374.0 0.0 reduce-scatter.11.cloned.1.call-update
  389.1 0.1 stack.83
  389.2 0.3 fusion.35
  389.5 0.1 stack.74
  389.6 65.4 %all-reduce = (f32[8]{0:T(128)}, f32[8]{0:T(128)}, f32[8,256]{1,0:T(8,128)}) all-reduce(f32[8]{0:T(128)S(1)} %stack.74, f32[8]{0:T(128)S(1)} %stack.83, f32[8,256]{1,0:T(8,128)S(1)} %fusion.35), channel_id=1, replica_groups=mesh['row'=16,'col'=8] {'row','col'}, use_global_device_ids=true, to_apply=%region_31.32 | all-reduce | flops 2064 | bytes 16512 | tf_op jit(solution)/shard_map/psum | solution.py:78
  454.9 1.6 copy.14
  456.5 637.7 %reduce-scatter.11.cloned.1.call-done = f32[8,256]{1,0:T(8,128)} async-done(((f32[1024,256]{1,0:T(8,128)}), f32[8,256]{1,0:T(8,128)}) %reduce-scatter.11.cloned.1.call-update) | async-done | bytes 8208 | tf_op jit(solution)/shard_map/reduce_scatter | solution.py:87
  (16 shorter events, 0.2 us)
Async XLA Ops:
  7.2 1.0 copy-start
  7.2 115.1 %copy-start.4 = (f32[8,256]{1,0:T(8,128)S(1)}, f32[8,256]{1,0:T(8,128)}, u32[]{:S(2)}) copy-start(f32[8,256]{1,0:T(8,128)} %param.15) | copy-start | bytes 24580
  7.2 120.3 %all-gather.2.cloned.1.call-start = ((), (), s32[]{:S(2)}) async-start(), calls=%async_computation.4 | async-start | bytes 1114112 | tf_op jit(solution)/shard_map/all_gather | solution.py:65
  13.1 279.8 %reduce-scatter.5.cloned.1.call-start = ((), (), s32[]{:S(2)}) async-start(), calls=%async_computation.5 | async-start | bytes 1179648 | tf_op jit(solution)/shard_map/reduce_scatter | solution.py:76
  129.8 23.8 %slice-start = ((s8[8388608]{0:T(1024)(128)(4,1)}), s8[4194304]{0:T(1024)(128)(4,1)S(1)}, s32[]{:S(2)}) async-start(s8[8388608]{0:T(1024)(128)(4,1)} %bitcast.108), calls=%async_computation.9 | async-start | bytes 8388608
  131.5 22.0 %slice-start.1 = ((s8[8388608]{0:T(1024)(128)(4,1)}), s8[4194304]{0:T(1024)(128)(4,1)S(1)}, s32[]{:S(2)}) async-start(s8[8388608]{0:T(1024)(128)(4,1)} %bitcast.108), calls=%async_computation.10 | async-start | bytes 8388608
  189.4 25.2 %copy-start.1 = (bf16[2048,256]{1,0:T(8,128)(2,1)S(1)}, bf16[2048,256]{1,0:T(8,128)(2,1)}, u32[]{:S(2)}) copy-start(bf16[2048,256]{1,0:T(8,128)(2,1)} %all-gather.2.cloned.1.call-done) | copy-start | bytes 3145732
  214.6 78.3 %copy-start.2 = (bf16[1024,256]{1,0:T(8,128)(2,1)S(1)}, bf16[1024,256]{1,0:T(8,128)(2,1)}, u32[]{:S(2)}) copy-start(bf16[1024,256]{1,0:T(8,128)(2,1)} %param.10) | copy-start | bytes 1572868
  223.1 149.5 %reduce-scatter.7.cloned.1.call-start = ((), (), s32[]{:S(2)}) async-start(), calls=%async_computation.6 | async-start | bytes 8912896 | tf_op jit(solution)/shard_map/reduce_scatter | solution.py:94
  292.9 79.8 %copy-start.3 = (f32[128,256]{1,0:T(8,128)S(1)}, f32[128,256]{1,0:T(8,128)}, u32[]{:S(2)}) copy-start(f32[128,256]{1,0:T(8,128)} %reduce-scatter.5.cloned.1.call-done) | copy-start | bytes 393220
  298.6 156.3 %reduce-scatter.9.cloned.1.call-start = ((), (), s32[]{:S(2)}) async-start(), calls=%async_computation.7 | async-start | bytes 589824 | tf_op jit(solution)/shard_map/reduce_scatter | solution.py:100
  372.6 721.5 %reduce-scatter.11.cloned.1.call-start = ((), (), s32[]{:S(2)}) async-start(), calls=%async_computation.8 | async-start | bytes 1056768 | tf_op jit(solution)/shard_map/reduce_scatter | solution.py:87
Sparse Core Ops, SparseCore 0:
  13.2 34.7 all-gather.1
  223.3 69.5 reduce-scatter.4
  298.8 73.8 reduce-scatter.6
  376.0 69.9 reduce-scatter.8
  448.7 645.4 reduce-scatter.10
where the time goes:
time: 1100 us
  waiting for transfers between devices  781 us (71%)
  blocking collectives  154 us (14%)
  other arithmetic  62.8 us (6%)
  matrix products  50.1 us (5%)
  between operations  44.2 us (4%)
    reduce_scatter x1, waiting for transfers between devices, body(): lax.psum_scatter(lax.dot_general(part, emb_cot, contract, preferred_eleme...  638 us
    reduce_scatter x1, waiting for transfers between devices, body(): lax.psum_scatter(lax.dot_general(part, d_hidden, contract, preferred_elem...  73.9 us
    reduce_scatter x1, waiting for transfers between devices, body(): lax.psum_scatter(partial_grad, 'col', scatter_dimension=0, tiled=True)  69.7 us
    psum x1, blocking collectives, body(): lax.psum((weights, varies, means), ('row', 'col'))  65.4 us
    all_gather x1, blocking collectives, body(): lax.all_gather(emb, 'col', axis=0, tiled=True)  36.2 us
    reduce_sum x2, other arithmetic, tile_terms(): varies.append(0.5 * mix_weight[comp] * -two_pi_sq * jnp.sum(even * dist))  35.7 us
    all_gather x1, blocking collectives, body(): lax.all_gather(factors, 'col', axis=0, tiled=True)  32.4 us
    reduce_sum x1, other arithmetic, tile_terms(): rowsum = jnp.sum(coef, 1)  25.1 us
  transfers between devices with their start and end apart: 5, of which 3 were waited for; matrix products, arithmetic and copies ran while one was open for 1% of the time, Pallas kernels for 0%

commit v1 on v0

v1 whole, which is shorter than its diff:
```python
import functools
import math

import jax
import jax.numpy as jnp
import numpy as np
from jax import lax
from jax.experimental import pallas as pl
from jax.experimental.pallas import tpu as pltpu
from jax.sharding import PartitionSpec as P


f32, bf16 = jnp.float32, jnp.bfloat16
NT = (((1,), (1,)), ((), ()))
NN = (((1,), (0,)), ((), ()))


def mm(a, b, dims):
    return lax.dot_general(a, b, dims, preferred_element_type=f32)


def split(x, n):
    out = []
    for _ in range(n):
        h = lax.reduce_precision(x, 8, 7)
        out.append(h.astype(bf16))
        x = x - h
    return out


def rates(mix_var):
    return (-2 * math.pi**2 * math.log2(math.e)) * mix_var


HI = lax.Precision.HIGHEST
TN = (((0,), (0,)), ((), ()))


def sel_matrix():
    m = np.zeros((256, 128), np.float32)
    for q in range(8):
        for t, at in enumerate((64, 72, 88, 96)):
            m[16*(q//4) + 4*t + q%4, at+q] = 1
        m[32+q, 72+q] = 1; m[40+q, 80+q] = 1; m[48+q, 96+q] = 1; m[56+q, 104+q] = 1
    m[64:72, 112:115] = 1
    m[128+115:128+118, :] = 1
    return m


def prep2(emb, fa, fb, mw, mv, mmean):
    ef = emb.astype(f32)
    ang = 2*math.pi*lax.dot_general(ef, mmean, NT, precision=HI)
    c, s = jnp.cos(ang), jnp.sin(ang)
    n = jnp.sum(ef*ef, 1, keepdims=True)
    nh, nm, nl = split(n, 3)
    one = jnp.ones((emb.shape[0], 3), bf16)
    a = mw * (-2*math.pi**2) * mv
    ch, cl = split(c, 2); sh, sl = split(s, 2)
    ah, al = split(c*a, 2); bh, bl = split(s*a, 2)
    z = jnp.zeros((emb.shape[0], 10), bf16)
    colp = jnp.concatenate([emb*-2, fa, fb, ch, cl, ch, sh, sl, sh, nh, nm, nl, one, z], 1)
    rowp = jnp.concatenate([emb, fb, fa, ah, ah, al, bh, bh, bl, one, nh, nm, nl, z], 1)
    return rowp, colp


def tile_kernel(TS, CE2, TR, TC, final, n_prev, rate_ref, sel_ref, mean_ref, row_ref, col_ref, *refs):
    prev, outs = refs[:n_prev], refs[n_prev:]
    if final:
        grad_ref, means_ref, v_ref = outs[:3]
    else:
        pulled_ref, rsum_ref, cs_ref, v_ref = outs[:4]
    outs = outs[3 if final else 4:]
    (rowc_s, d0, d1, o0, o1, m0, m1, c0, c1, pulled_s, rsum_s, cs_s, cst_s, ni_s, nj_s) = outs
    HW = 128
    R, C = row_ref.shape[0], col_ref.shape[0]
    Q = rate_ref.shape[0]
    NC, NR = C // TC, R // TR
    N = NC * NR
    NS = TR // TS
    CW = min(TC, 256)
    lane = lax.broadcasted_iota(jnp.int32, (TS, 128), 1)

    def zero(*refs):
        for r in refs:
            r[...] = jnp.zeros_like(r)

    zero(d0, d1, o0, o1, m0, m1, c0, c1)
    if final:
        zero(means_ref)

    def load_sums(i):
        if prev:
            rows = pl.ds(pl.multiple_of(i * TR, TR), TR)
            pulled_s[...] = prev[0][rows, :]
            rsum_s[...] = prev[1][rows, :]
            cs_s[...] = prev[2][i]
        else:
            zero(pulled_s, rsum_s, cs_s)

    load_sums(0)
    if prev:
        v_ref[...] = prev[3][...]
    else:
        zero(v_ref)
    lr = lax.broadcasted_iota(jnp.int32, (TR, 128), 1)
    sub = lax.broadcasted_iota(jnp.int32, (16, TC), 0)

    def rowcol(t):
        t = jnp.clip(t, 0, N - 1)
        i, j = lax.div(t, NC), lax.rem(t, NC)
        return pl.multiple_of(i * TR, TR), pl.multiple_of(j * TC, TC)

    def products(t, d_s, o_s):
        r0, q0 = rowcol(t)
        cols = pl.ds(q0, TC)
        rows = pl.ds(r0, TR)

        def dist():
            norms = jnp.concatenate([ni_s[rows, :]] * (TC // 128), 1) + nj_s[0:1, cols]
            d_s[...] = norms + mm(row_ref[rows, :256], col_ref[cols, :256], NT)

        def outer():
            rtail = row_ref[rows, 256:384]
            keep = jnp.where((lr < 64) & (t < N), rtail, jnp.zeros_like(rtail))
            o_s[...] = mm(keep, col_ref[cols, 256:384], NT)

        return [dist, outer]

    def sums(t, damp_s, c_s):
        _, q0 = rowcol(t)
        cols = pl.ds(q0, TC)
        acc = [None, None]

        def waves(q):
            r = mm(cst_s[q, :, cols], damp_s[q], NT)
            h = q // 4
            acc[h] = r if acc[h] is None else acc[h] + r
            if q % 4 == 3:
                cs_s[16*h:16*h+16] += acc[h]

        def pull(h):
            M = TR
            rows = slice(h * M, (h + 1) * M)
            emb = col_ref[cols, :256]
            c = c_s[rows, :]
            chi = c.astype(bf16)
            pu = mm(chi, emb, NN)
            if CE2:
                pu = pu + mm((c - chi.astype(f32)).astype(bf16), emb, NN)
            pulled_s[rows, :] += pu
            rs = c[:, :128]
            for k in range(1, TC // 128):
                rs = rs + c[:, k*128:(k+1)*128]
            rsum_s[rows, :] += rs

        return [functools.partial(waves, q) for q in range(Q)], [functools.partial(pull, h) for h in range(1)]

    def stage(t, da, oa, ds, os, ms, cs, mc, cc_):
        first = products(t, da, oa)
        waves, pulls = sums(t - 2, mc, cc_)
        r0, q0 = rowcol(t - 1)
        for s in range(NS):
            rs = slice(s * TS, (s + 1) * TS)
            lhs = rowc_s[pl.ds(pl.multiple_of((r0 + s * TS) * Q, TS * Q), Q*TS), :]
            for cc in range(TC // CW):
                cos = mm(lhs, col_ref[pl.ds(q0 + cc*CW, CW), 256:384], NT)
                for hh in range(CW // HW):
                    sl = slice(hh*HW, (hh+1)*HW)
                    hcols = slice(cc*CW + hh*HW, cc*CW + (hh+1)*HW)
                    d = ds[rs, hcols]
                    o = os[rs, hcols]
                    c = None
                    for q in range(Q):
                        damp = o * jnp.exp2(d * rate_ref[q])
                        ms[q, rs, hcols] = damp.astype(bf16)
                        even = damp * cos[q*TS:(q+1)*TS, sl]
                        c = even if c is None else c + even
                        ed = even * d
                        x = ed[:, :128]
                        for k in range(1, HW // 128):
                            x = x + ed[:, k*128:(k+1)*128]
                        x = x.reshape(TS//8, 8, 128).sum(0)
                        v_ref[q] += x
                        v_ref[Q + q] += even.reshape(TS//8, 8, 128).sum(0)
                    cs[rs, hcols] = c
            for _ in range(-(-Q // NS)):
                if waves:
                    waves.pop(0)()
            if s % max(1, NS // 2) == 0 and first:
                first.pop(0)()
            if (s % max(1, NS // 2) == 1 or NS == 2) and pulls:
                pulls.pop(0)()
        for f in first + waves + pulls:
            f()

    def end_rows(t):
        @pl.when((t >= 0) & (lax.rem(t, NC) == NC - 1))
        def _():
            r0, _ = rowcol(t)
            rows = pl.ds(r0, TR)
            if final:
                ef = row_ref[rows, :256].astype(f32)
                cs = cs_s[...]
                wc = jnp.concatenate([cs[0:4] + cs[4:8], cs[16:20] + cs[20:24]], 0)
                ws = jnp.concatenate([cs[8:12] + cs[12:16], cs[24:28] + cs[28:32]], 0)
                rt = mm(sel_ref[32:64], row_ref[rows, 256:384], NT)
                ac = rt[0:8] + rt[8:16]
                as_ = rt[16:24] + rt[24:32]
                spin = as_ * wc - ac * ws
                rowsum = jnp.sum(rsum_s[...], 1, keepdims=True)
                back = lax.dot_general(spin, mean_ref[...], TN, precision=HI, preferred_element_type=f32)
                grad_ref[rows, :] = (2.0 * rowsum * ef + pulled_s[...] + back).astype(grad_ref.dtype)
                means_ref[...] += lax.dot_general(spin, ef, NN, precision=HI, preferred_element_type=f32)
            else:
                pulled_ref[rows, :] = pulled_s[...]
                rsum_ref[rows, :] = rsum_s[...]
                cs_ref[lax.div(t, NC)] = cs_s[...]
            load_sums(jnp.minimum(lax.div(t, NC) + 1, NR - 1))

    for s in range(R // TS):
        x = row_ref[s*TS:(s+1)*TS, 256:384]
        for q in range(Q):
            keep = (lane >= 64) & (lane < 112) & (lane % 8 == q)
            rowc_s[(s*Q+q)*TS:(s*Q+q+1)*TS, :] = jnp.where(keep, x, jnp.zeros_like(x))
    for k in range(C // TC):
        cst = mm(sel_ref[:32], col_ref[k*TC:(k+1)*TC, 256:384], NT)
        for q in range(Q):
            keep = cst[16*(q//4):16*(q//4)+16]
            cst_s[q, :, k*TC:(k+1)*TC] = jnp.where(sub % 4 == q % 4, keep, 0.0).astype(bf16)
        nj_s[:, k*TC:(k+1)*TC] = mm(sel_ref[64:72], col_ref[k*TC:(k+1)*TC, 256:384], NT)
    for k in range(R // TR):
        ni_s[k*TR:(k+1)*TR, :] = mm(row_ref[k*TR:(k+1)*TR, 256:384], sel_ref[128:256], NN)

    def pair(h, _):
        t = 2 * h
        stage(t, d0, o0, d1, o1, m1, c1, m0, c0)
        stage(t + 1, d1, o1, d0, o0, m0, c0, m1, c1)
        end_rows(t - 1)
        return 0

    lax.fori_loop(0, (N + 2) // 2, pair, 0)


def tile(rate, mean_s, rowp, colp, prev=(), final=True, TR=256, TC=256, TS=64, CE2=False):
    R, C, Q = rowp.shape[0], colp.shape[0], rate.shape[0]
    assert (R // TR) * (C // TC) % 2 == 0
    vm = pl.BlockSpec(memory_space=pltpu.VMEM)
    sc = lambda *s: pltpu.VMEM(s, f32)
    shape = lambda *dims: jax.ShapeDtypeStruct(dims, f32)
    if final:
        shapes = [shape(R, 256), shape(8, 256), shape(2 * Q, 8, 128)]
    else:
        shapes = [shape(R, 256), shape(R, 128), shape(R // TR, 32, TR), shape(2 * Q, 8, 128)]
    return pl.pallas_call(
        functools.partial(tile_kernel, TS, CE2, TR, TC, final, len(prev)),
        in_specs=[pl.BlockSpec(memory_space=pltpu.SMEM), vm, vm, vm, vm] + [vm] * len(prev),
        out_specs=[vm] * len(shapes),
        out_shape=shapes,
        scratch_shapes=[pltpu.VMEM((R*Q, 128), bf16), sc(TR, TC), sc(TR, TC), sc(TR, TC), sc(TR, TC),
                        pltpu.VMEM((Q, TR, TC), bf16), pltpu.VMEM((Q, TR, TC), bf16), sc(TR, TC), sc(TR, TC),
                        sc(TR, 256), sc(TR, 128), sc(32, TR), pltpu.VMEM((Q, 16, C), bf16), sc(R, 128), sc(8, C)],
        cost_estimate=pl.CostEstimate(flops=20 * R * C * 256, bytes_accessed=4 * 10**6, transcendentals=R * C * Q),
        compiler_params=pltpu.CompilerParams(vmem_limit_bytes=20 << 20),
        name="tile",
    )(rate, jnp.asarray(sel_matrix(), bf16), mean_s, rowp, colp, *prev)


def pre_kernel(w_ref, wh_ref, *refs):
    pieces, (slope_ref, hid_ref) = refs[:-2], refs[-2:]
    for p in range(0, len(pieces), 2):
        two = jnp.concatenate([pieces[p][...], pieces[p+1][...]], 0)
        n = two.shape[0]
        cols = slice(p * n // 2, (p + 2) * n // 2)
        pre = mm(two, w_ref[...], NN)
        sig = jax.nn.sigmoid(pre)
        slope_ref[:, cols] = (sig * (1.0 + pre * (1.0 - sig))).T
        pre = mm(two, wh_ref[...], NN)
        hid_ref[:, cols] = (pre * jax.nn.sigmoid(pre)).T.astype(bf16)


def late_pre(w_own, w_pick, pieces):
    vm = pl.BlockSpec(memory_space=pltpu.VMEM)
    tok = sum(p.shape[0] for p in pieces)
    return pl.pallas_call(
        pre_kernel,
        in_specs=[vm] * (2 + len(pieces)),
        out_specs=[vm, vm],
        out_shape=[jax.ShapeDtypeStruct((w_own.shape[1], tok), f32), jax.ShapeDtypeStruct((w_pick.shape[1], tok), bf16)],
        cost_estimate=pl.CostEstimate(flops=4 * 10**9, bytes_accessed=6 * 10**6, transcendentals=400000),
        compiler_params=pltpu.CompilerParams(vmem_limit_bytes=20 << 20),
        name="pre",
    )(w_own, w_pick, *pieces)


def pair_split(x):
    h = x.astype(bf16)
    return h, (x - h.astype(f32)).astype(bf16)


def part_kernel(own, n, at_ref, slope_ref, hid_ref, w_ref, *refs):
    cots, pieces, (out_ref,) = refs[:n], refs[n:2*n], refs[2*n:]
    core, x, y, z = at_ref[0], at_ref[1], at_ref[2], at_ref[3]
    wide = slope_ref.shape[0]
    cot = jnp.concatenate([c[:own, :] for c in cots], 0)
    small = cots[0][own:own+16, :].astype(f32) + cots[0][own+16:own+32, :].astype(f32)
    for c in cots[1:]:
        small = small + (c[own:own+16, :].astype(f32) + c[own+16:own+32, :].astype(f32))
    hi, lo = pair_split(small)
    for k, part in enumerate((hi, lo)):
        for dest in range(4):
            out_ref[dest, 576+32*k:592+32*k, :] = part[:, :128]
            out_ref[dest, 592+32*k:608+32*k, :] = part[:, 128:]
    back = mm(w_ref[pl.ds(pl.multiple_of(z * wide, wide), wide), :], cot, NT)
    d = (back * slope_ref[...]).astype(bf16)
    grad_out = mm(hid_ref[...], cot, NN)
    for m in range(8):
        feats = pl.ds(pl.multiple_of((2 * m + core) * 128, 128), 128)
        g = mm(d, jnp.concatenate([p[:, feats] for p in pieces], 0), NN)
        sx = lax.rem(m % 4 - x + 4, 4)
        for h in range(2):
            sy = lax.rem(2 * h + m // 4 - y + 4, 4)
            base = pl.multiple_of(sy * 144, 16)
            out_ref[sx, pl.ds(base, 128), :] = g[h*128:(h+1)*128].astype(bf16)
            o = grad_out[16*m+8*h:16*m+8*h+8]
            out_ref[sx, pl.ds(base + 128, 16), :] = jnp.concatenate([o[:, :128], o[:, 128:]], 0).astype(bf16)


def late_part(at, slope, hid_out, w_out, cots, pieces):
    vm = pl.BlockSpec(memory_space=pltpu.VMEM)
    n = len(pieces)
    return pl.pallas_call(
        functools.partial(part_kernel, pieces[0].shape[0], n),
        in_specs=[pl.BlockSpec(memory_space=pltpu.SMEM)] + [vm] * (3 + 2 * n),
        out_specs=vm,
        out_shape=jax.ShapeDtypeStruct((4, 640, 128), bf16),
        cost_estimate=pl.CostEstimate(flops=2 * 10**9, bytes_accessed=6 * 10**6, transcendentals=0),
        compiler_params=pltpu.CompilerParams(vmem_limit_bytes=20 << 20),
        name="part",
    )(at, slope, hid_out, w_out, *cots, *pieces)


def add_kernel(first_ref, *refs):
    got, out_ref = refs[:3], refs[3]
    for dest in range(4):
        rows = slice(144 * dest, 144 * dest + 144)
        total = first_ref[0, rows].astype(f32)
        for g in got:
            total = total + g[rows].astype(f32)
        out_ref[dest, :144, :] = total.astype(bf16)
    value = first_ref[0, 576:608].astype(f32) + first_ref[0, 608:640].astype(f32)
    for g in got:
        value = value + (g[576:608].astype(f32) + g[608:640].astype(f32))
    hi, lo = pair_split(value)
    for dest in range(4):
        out_ref[dest, 144:176, :] = hi
        out_ref[dest, 176:208, :] = lo


def x_sum(out, got):
    vm = pl.BlockSpec(memory_space=pltpu.VMEM)
    return pl.pallas_call(
        add_kernel,
        grid=(1,),
        in_specs=[pl.BlockSpec((1, 640, 128), lambda i: (0, 0, 0))] + [vm] * 3,
        out_specs=vm,
        out_shape=jax.ShapeDtypeStruct((4, 208, 128), bf16),
        compiler_params=pltpu.CompilerParams(vmem_limit_bytes=6 << 20),
        name="x_sum",
    )(out, *got)


def end_kernel(first_ref, *refs):
    got, (in_ref, out_ref, weight_ref, var_ref, mean_ref) = refs[:3], refs[3:]
    total = first_ref[0].astype(f32)
    for g in got:
        total = total + g[...].astype(f32)
    in_ref[...] = total[:128].T
    out_ref[:, :128] = total[128:136]
    out_ref[:, 128:] = total[136:144]
    value = total[144:176] + total[176:208]
    mean_ref[:, :128] = value[:8]
    mean_ref[:, 128:] = value[16:24]
    weight_ref[...] = value[8, :8]
    var_ref[...] = value[8, 8:16]


def y_sum(out, got):
    vm = pl.BlockSpec(memory_space=pltpu.VMEM)
    return pl.pallas_call(
        end_kernel,
        grid=(1,),
        in_specs=[pl.BlockSpec((1, 208, 128), lambda i: (0, 0, 0))] + [vm] * 3,
        out_specs=[vm] * 5,
        out_shape=[jax.ShapeDtypeStruct((128, 128), f32), jax.ShapeDtypeStruct((8, 256), f32), jax.ShapeDtypeStruct((8,), f32),
                   jax.ShapeDtypeStruct((8,), f32), jax.ShapeDtypeStruct((8, 256), f32)],
        compiler_params=pltpu.CompilerParams(vmem_limit_bytes=6 << 20),
        name="y_sum",
    )(out, *got)


BOTH = ("row", "col")


def device_at(core, x, y, z):
    x, y, z = x % 4, y % 4, z % 4
    return (((y % 2) * 4 + x) * 2 + core) * 8 + z * 2 + y // 2


def shift(v, dx=0, dy=0, dz=0, swap=0):
    pairs = [(device_at(k, x, y, z), device_at(k ^ swap, x + dx, y + dy, z + dz))
             for k in range(2) for x in range(4) for y in range(4) for z in range(4)]
    return lax.ppermute(v, BOTH, sorted(pairs))


def body(series, w_in, w_out, factor_a, factor_b, mix_weight, mix_var, mix_mean):
    row, col = lax.axis_index("row"), lax.axis_index("col")
    core, x, z = lax.rem(row, 2), lax.rem(lax.div(row, 2), 4), lax.div(col, 2)
    y = 2 * lax.rem(col, 2) + lax.div(row, 8)
    at = jnp.stack([core, x, y, z]).astype(jnp.int32)
    pre = jnp.dot(series, w_in, preferred_element_type=f32)
    hidden = jax.nn.silu(pre).astype(bf16)
    emb = jnp.dot(hidden, w_out, preferred_element_type=f32).astype(bf16)
    rowp, colp = prep2(emb, factor_a, factor_b, mix_weight, mix_var, mix_mean)
    near = jnp.concatenate([colp] + [shift(colp, dy=d) for d in (1, 2, 3)], 0)
    near, rowp = lax.optimization_barrier((near, rowp))
    rows = [shift(rowp, dz=d) for d in (1, 2, 3)]
    rows = jnp.concatenate([rowp] + rows, 0)
    rows, series_late = lax.optimization_barrier((rows, series))
    series_z = [series_late] + [shift(series_late, dz=d) for d in (1, 2, 3)]
    rows = jnp.concatenate([rows, shift(rows, swap=1)], 0)
    far = [shift(near, dx=d) for d in (1, 2, 3)]
    far = jnp.concatenate(far, 0)
    inv = 1.0 / (math.pi * mix_var)
    rate, mean_s = rates(mix_var), mix_mean * inv[:, None]
    sums = tile(rate, mean_s, rows, near, final=False)
    rows, far, sums = lax.optimization_barrier((rows, far, sums))
    part, means, v = tile(rate, mean_s, rows, far, prev=sums)
    series_z, part = lax.optimization_barrier((series_z, part))
    half = part.shape[0] // 2
    part = (part[:half] + shift(part[half:], swap=1)).reshape(4, -1, 256)
    part, w_in_late = lax.optimization_barrier((part, w_in))
    grad_embed = part[0]
    for d in (1, 2, 3):
        grad_embed = grad_embed + shift(part[d].astype(bf16), dz=-d).astype(f32)
    emb_cot = grad_embed.astype(bf16)
    small = jnp.concatenate(
        [
            means * inv[:, None],
            jnp.concatenate([0.5 * jnp.sum(v[8:], (1, 2)) / (mix_weight * mix_var * (-2 * math.pi**2)),
                             0.5 / mix_var * jnp.sum(v[:8], (1, 2)), jnp.zeros((240,), f32)])[None],
            jnp.zeros((7, 256), f32),
        ],
        0,
    )
    series_all = series_z + [shift(s, swap=1) for s in series_z]
    hid = w_in.shape[1]
    wide = hid // 4
    k = jnp.arange(hid // 8)
    ids = (2 * (k // 16) + core) * 64 + z * 16 + k % 16
    pick = (jnp.arange(hid)[:, None] == ids[None, :]).astype(bf16)
    w_pick = jnp.dot(w_in_late, pick, preferred_element_type=f32).astype(bf16)
    w_own = lax.dynamic_slice_in_dim(w_in_late, z * wide, wide, 1)
    slope, hid_out = late_pre(w_own, w_pick, series_all)
    sent = jnp.concatenate([emb_cot, *split(small, 2)], 0)
    cots = [sent] + [shift(sent, dz=d) for d in (1, 2, 3)]
    cots, slope, hid_out = lax.optimization_barrier((cots, slope, hid_out))
    cots = cots + [shift(c, swap=1) for c in cots]
    out = late_part(at, slope, hid_out, w_out, cots, series_all)
    out = x_sum(out, [shift(out[d], dx=d) for d in (1, 2, 3)])
    grad_in, grad_out, weights, varies, means = y_sum(out, [shift(out[d], dy=d) for d in (1, 2, 3)])
    return (grad_embed, grad_in, grad_out, weights, varies, means)


def solution(mesh):
    both = P(("row", "col"), None)
    return jax.shard_map(
        body,
        mesh=mesh,
        in_specs=(both, P(), P(), both, both, P(), P(), P()),
        out_specs=(both, P("row", "col"), both, P(), P(), P()),
        check_vma=False,
    )
```

time: 1100 us -> 131 us (0.12)
  waiting for transfers between devices: 781 us -> 46 us
  blocking collectives: 154 us -> 0 us
  other arithmetic: 62.8 us -> 1.71 us
  matrix products: 50.1 us -> 5.09 us
  between operations: 44.2 us -> 1.02 us
  Pallas kernels: 0 us -> 40.4 us
  starting transfers between devices: 0.2 us -> 34.1 us
    reduce_scatter x4 -> x0, waiting for transfers between devices: 781 us -> none  [the longest x1 638 us: body(): lax.psum_scatter(lax.dot_general(part, emb_cot, contract, preferred_eleme...]
    all_gather x3 -> x0, blocking collectives: 89 us -> none  [the longest x1 36.2 us: body(): lax.all_gather(emb, 'col', axis=0, tiled=True)]
    psum x1 -> x0, blocking collectives: 65.4 us -> none  [body(): lax.psum((weights, varies, means), ('row', 'col'))]
    reduce_sum x5 -> x2, other arithmetic: 62.7 us -> 0.24 us  [the longest x1 0.14 us: body(): jnp.sum(v[8:], (1, 2))]
    ppermute x0 -> x34, waiting for transfers between devices: none -> 46 us  [shift(): return lax.ppermute(v, BOTH, sorted(pairs))]
    dot_general x11 -> x3, matrix products: 50.1 us -> 5.09 us  [the longest x1 3.42 us: body(): emb = jnp.dot(hidden, w_out, preferred_element_type=f32).astype(bf16)]
    pallas_call x0 -> x6, Pallas kernels: none -> 40.4 us  [the longest x2 34.9 us: tile(): pl.pallas_call(functools.partial(tile_kernel, TS, CE2, TR, TC, final, len...]
    ppermute x0 -> x34, starting transfers between devices: none -> 34.1 us  [shift(): return lax.ppermute(v, BOTH, sorted(pairs))]
  transfers between devices with their start and end apart: 5 -> 34, of which waited for: 3 -> 23; matrix products, arithmetic and copies ran while one was open for 1% -> 3% of each run, Pallas kernels for 0% -> 29%
where the time goes in v1:
time: 131 us
  waiting for transfers between devices  46 us (35%)
  Pallas kernels  40.4 us (31%)
  starting transfers between devices  34.1 us (26%)
  matrix products  5.09 us (4%)
  local copies, waits for them, and re-layouts  2.71 us (2%)
  other arithmetic  1.71 us (1%)
    ppermute x34, waiting for transfers between devices, shift(): return lax.ppermute(v, BOTH, sorted(pairs))  46 us
    pallas_call x2, Pallas kernels, tile(): pl.pallas_call(functools.partial(tile_kernel, TS, CE2, TR, TC, final, len...  34.9 us
    ppermute x34, starting transfers between devices, shift(): return lax.ppermute(v, BOTH, sorted(pairs))  34.1 us
    dot_general x1, matrix products, body(): emb = jnp.dot(hidden, w_out, preferred_element_type=f32).astype(bf16)  3.42 us
  transfers between devices with their start and end apart: 34, of which 23 were waited for; matrix products, arithmetic and copies ran while one was open for 3% of the time, Pallas kernels for 29%

profile of v1, /device:TPU:0, one launch (start us, length us, event | category | flops | bytes accessed | tf_op | source)
XLA Modules:
  0.0 131.0 jit_solution(11247552296883164670)
XLA Ops:
  0.6 0.8 copy.28
  1.4 0.8 copy.29
  2.3 3.4 %broadcast_multiply_fusion = (bf16[128,256]{1,0:T(8,128)(2,1)S(1)}, bf16[128,256]{1,0:T(8,128)(2,1)S(1)}) fusion(bf16[1024,256]{1,0:T(8,128)(2,1)} %w_ref.1, bf16[128,2048]{1,0:T(8,128)(2,1)} %refs_8_, bf16[2048,1024]{1,0:T(8,128)(2,1)} %param.11), kind=kOutput, calls=%fused_computation.47 | convolution fusion | flops 604798976 | bytes 5373952 | tf_op jit(solution)/shard_map/dot_general | solution.py:422
  6.8 3.2 %collective-permute-start.2 = (bf16[128,384]{1,0:T(8,128)(2,1)S(1)}, bf16[128,384]{1,0:T(8,128)(2,1)S(1)}, u32[]{:S(2)}, u32[]{:S(2)}) collective-permute-start(bf16[128,384]{1,0:T(8,128)(2,1)S(1)} %concatenate.27), channel_id=1, source_target_pairs={{0,65},{1,64},{2,67},{3,66},{4,69},{5,68},{6,71},{7,70},{8,73},{9,... | collective-permute-start | bytes 294920 | tf_op jit(solution)/shard_map/ppermute | solution.py:412
  10.0 0.6 collective-permute-start.1
  10.7 1.0 collective-permute-start
  11.8 2.4 %collective-permute-done.2 = bf16[128,384]{1,0:T(8,128)(2,1)S(1)} collective-permute-done((bf16[128,384]{1,0:T(8,128)(2,1)S(1)}, bf16[128,384]{1,0:T(8,128)(2,1)S(1)}, u32[]{:S(2)}, u32[]{:S(2)}) %collective-permute-start.2) | collective-permute-done | bytes 98336 | tf_op jit(solution)/shard_map/ppermute | solution.py:412
  14.2 2.6 %collective-permute-done.1 = bf16[128,384]{1,0:T(8,128)(2,1)S(1)} collective-permute-done((bf16[128,384]{1,0:T(8,128)(2,1)S(1)}, bf16[128,384]{1,0:T(8,128)(2,1)S(1)}, u32[]{:S(2)}, u32[]{:S(2)}) %collective-permute-start.1) | collective-permute-done | bytes 98336 | tf_op jit(solution)/shard_map/ppermute | solution.py:412
  16.9 1.1 collective-permute-done
  18.0 4.1 %collective-permute-start.5 = (bf16[128,384]{1,0:T(8,128)(2,1)S(1)}, bf16[128,384]{1,0:T(8,128)(2,1)S(1)}, u32[]{:S(2)}, u32[]{:S(2)}) collective-permute-start(bf16[128,384]{1,0:T(8,128)(2,1)S(1)} %concatenate.29), channel_id=1, source_target_pairs={{0,6},{1,7},{2,0},{3,1},{4,2},{5,3},{6,4},{7,5},{8,14},{9,15},{10,... | collective-permute-start | bytes 294920 | tf_op jit(solution)/shard_map/ppermute | solution.py:412
  22.1 1.3 collective-permute-start.3
  23.3 2.7 %collective-permute-start.12 = (bf16[512,384]{1,0:T(8,128)(2,1)S(1)}, bf16[512,384]{1,0:T(8,128)(2,1)S(1)}, u32[]{:S(2)}, u32[]{:S(2)}) collective-permute-start(bf16[512,384]{1,0:T(8,128)(2,1)S(1)} %pad_maximum_fusion.1.col_ref), channel_id=1, source_target_pairs={{0,48},{1,49},{2,50},{3,51},{4,52},{5,53},{6,54},{7,55},{8,56},{9,... | collective-permute-start | bytes 1179656 | tf_op jit(solution)/shard_map/ppermute | solution.py:412
  26.1 0.8 collective-permute-start.11
  26.9 0.9 collective-permute-start.10
  27.8 0.8 collective-permute-done.4
  28.7 0.7 collective-permute-done.3
  29.7 1.9 %collective-permute-start.8 = (bf16[128,2048]{1,0:T(8,128)(2,1)S(1)}, bf16[128,2048]{1,0:T(8,128)(2,1)S(1)}, u32[]{:S(2)}, u32[]{:S(2)}) collective-permute-start(bf16[128,2048]{1,0:T(8,128)(2,1)S(1)} %copy-done.1), channel_id=1, source_target_pairs={{0,6},{1,7},{2,0},{3,1},{4,2},{5,3},{6,4},{7,5},{8,14},{9,15},{10,... | collective-permute-start | bytes 1572872 | tf_op jit(solution)/shard_map/ppermute | solution.py:412
  31.6 10.3 %collective-permute-done.12 = bf16[512,384]{1,0:T(8,128)(2,1)S(1)} collective-permute-done((bf16[512,384]{1,0:T(8,128)(2,1)S(1)}, bf16[512,384]{1,0:T(8,128)(2,1)S(1)}, u32[]{:S(2)}, u32[]{:S(2)}) %collective-permute-start.12) | collective-permute-done | bytes 393248 | tf_op jit(solution)/shard_map/ppermute | solution.py:412
  41.8 2.6 %collective-permute-start.7 = (bf16[128,2048]{1,0:T(8,128)(2,1)S(1)}, bf16[128,2048]{1,0:T(8,128)(2,1)S(1)}, u32[]{:S(2)}, u32[]{:S(2)}) collective-permute-start(bf16[128,2048]{1,0:T(8,128)(2,1)S(1)} %copy-done.1), channel_id=1, source_target_pairs={{0,4},{1,5},{2,6},{3,7},{4,0},{5,1},{6,2},{7,3},{8,12},{9,13},{10,... | collective-permute-start | bytes 1572872 | tf_op jit(solution)/shard_map/ppermute | solution.py:412
  44.4 0.6 collective-permute-start.6
  45.0 0.5 collective-permute-done.10
  45.7 9.7 %tile.2 = (f32[1024,256]{1,0:T(8,128)S(1)}, f32[1024,128]{1,0:T(8,128)S(1)}, f32[4,32,256]{2,1,0:T(8,128)S(1)}, f32[16,8,128]{2,1,0:T(8,128)S(1)}) custom-call(f32[8]{0:T(128)S(1)} %get-tuple-element.111.rate_ref, bf16[256,128]{1,0:T(8,128)(2,1)S(1)} %copy-done.2, f32[8,256]{1,0:T(8,128)S(1)} %broadcast_multiply_fusion.2.mean_ref, ...), custom_call_target="tpu_custom_call" | custom-call | flops 2684354560 | bytes 4000000 | tf_op jit(solution)/shard_map/tile/pallas_call | solution.py:254
  55.4 25.2 %tile.3 = (f32[1024,256]{1,0:T(8,128)S(1)}, f32[8,256]{1,0:T(8,128)S(1)}, f32[16,8,128]{2,1,0:T(8,128)S(1)}) custom-call(f32[8]{0:T(128)S(1)} %get-tuple-element.111.rate_ref, bf16[256,128]{1,0:T(8,128)(2,1)S(1)} %copy-done.2, f32[8,256]{1,0:T(8,128)S(1)} %broadcast_multiply_fusion.2.mean_ref, ...), custom_call_target="tpu_custom_call" | custom-call | flops 8053063680 | bytes 4000000 | tf_op jit(solution)/shard_map/tile/pallas_call | solution.py:254
  82.2 0.6 collective-permute-done.13
  83.0 2.4 %collective-permute-start.14 = (bf16[128,256]{1,0:T(8,128)(2,1)S(1)}, bf16[128,256]{1,0:T(8,128)(2,1)S(1)}, u32[]{:S(2)}, u32[]{:S(2)}) collective-permute-start(bf16[128,256]{1,0:T(8,128)(2,1)S(1)} %get-tuple-element.87), channel_id=1, source_target_pairs={{0,6},{1,7},{2,0},{3,1},{4,2},{5,3},{6,4},{7,5},{8,14},{9,15},{10,... | collective-permute-start | bytes 196616 | tf_op jit(solution)/shard_map/ppermute | solution.py:412
  85.4 1.3 convolution_convert_fusion.wh_ref
  86.7 1.0 collective-permute-done.14
  87.7 3.1 %collective-permute-done.16 = bf16[128,256]{1,0:T(8,128)(2,1)S(1)} collective-permute-done((bf16[128,256]{1,0:T(8,128)(2,1)S(1)}, bf16[128,256]{1,0:T(8,128)(2,1)S(1)}, u32[]{:S(2)}, u32[]{:S(2)}) %collective-permute-start.16) | collective-permute-done | bytes 65568 | tf_op jit(solution)/shard_map/ppermute | solution.py:412
  90.8 0.8 collective-permute-start.15
  91.8 4.8 %collective-permute-done.15 = bf16[128,256]{1,0:T(8,128)(2,1)S(1)} collective-permute-done((bf16[128,256]{1,0:T(8,128)(2,1)S(1)}, bf16[128,256]{1,0:T(8,128)(2,1)S(1)}, u32[]{:S(2)}, u32[]{:S(2)}) %collective-permute-start.15) | collective-permute-done | bytes 65568 | tf_op jit(solution)/shard_map/ppermute | solution.py:412
  96.6 0.7 fusion.22
  97.6 0.8 collective-permute-start.18
  98.5 1.3 collective-permute-start.17
  99.7 2.5 %pre.1 = (f32[256,1024]{1,0:T(8,128)S(1)}, bf16[128,1024]{1,0:T(8,128)(2,1)S(1)}) custom-call(bf16[2048,256]{1,0:T(8,128)(2,1)S(1)} %constant_dynamic-slice_fusion.w_ref, bf16[2048,128]{1,0:T(8,128)(2,1)S(1)} %convolution_convert_fusion.wh_ref, bf16[128,2048]{1,0:T(8,128)(2,1)S(1)} %copy-done.1, ...), custom_call_target="tpu_custom_call" | custom-call | flops 4000000000 | bytes 6000000 | tf_op jit(solution)/shard_map/pre/pallas_call | solution.py:284
  102.2 1.5 %collective-permute-done.18.refs_2_ = bf16[160,256]{1,0:T(8,128)(2,1)S(1)} collective-permute-done((bf16[160,256]{1,0:T(8,128)(2,1)S(1)}, bf16[160,256]{1,0:T(8,128)(2,1)S(1)}, u32[]{:S(2)}, u32[]{:S(2)}) %collective-permute-start.18) | collective-permute-done | bytes 81952 | tf_op jit(solution)/shard_map/ppermute | solution.py:412
  103.7 0.9 collective-permute-done.17.refs_1_
  104.6 0.5 collective-permute-start.25
  106.6 2.2 %part.1.first_ref = bf16[4,640,128]{2,1,0:T(8,128)(2,1)S(1)} custom-call(s32[4]{0:T(128)S(1)} %pad_add_fusion.at_ref, f32[256,1024]{1,0:T(8,128)S(1)} %get-tuple-element.69.slope_ref, bf16[128,1024]{1,0:T(8,128)(2,1)S(1)} %get-tuple-element.70.hid_ref, bf16[1024,256]{1,0:T(8,128)(2,1)S(1)} %copy-done, bf16[160,256]{1,0:T(8,128)(2,1)S(1)} %pad_maximum_fusion.3.refs_0_, ...), custom_call_target="tpu_custom_call" | custom-call | flops 2000000000 | bytes 6000000 | tf_op jit(solution)/shard_map/part/pallas_call | solution.py:331
  108.8 3.6 %collective-permute-start.30 = (bf16[640,128]{1,0:T(8,128)(2,1)S(1)}, bf16[640,128]{1,0:T(8,128)(2,1)S(1)}, u32[]{:S(2)}, u32[]{:S(2)}) collective-permute-start(bf16[640,128]{1,0:T(8,128)(2,1)S(1)} %get-tuple-element.84), channel_id=1, source_target_pairs={{0,48},{1,49},{2,50},{3,51},{4,52},{5,53},{6,54},{7,55},{8,56},{9,... | collective-permute-start | bytes 491528 | tf_op jit(solution)/shard_map/ppermute | solution.py:412
  112.4 0.9 collective-permute-start.28
  113.3 6.5 %collective-permute-done.30.refs_2_ = bf16[640,128]{1,0:T(8,128)(2,1)S(1)} collective-permute-done((bf16[640,128]{1,0:T(8,128)(2,1)S(1)}, bf16[640,128]{1,0:T(8,128)(2,1)S(1)}, u32[]{:S(2)}, u32[]{:S(2)}) %collective-permute-start.30) | collective-permute-done | bytes 163872 | tf_op jit(solution)/shard_map/ppermute | solution.py:412
  119.9 1.1 collective-permute-done.29.refs_1_
  121.0 2.3 %collective-permute-done.28.refs_0_ = bf16[640,128]{1,0:T(8,128)(2,1)S(1)} collective-permute-done((bf16[640,128]{1,0:T(8,128)(2,1)S(1)}, bf16[640,128]{1,0:T(8,128)(2,1)S(1)}, u32[]{:S(2)}, u32[]{:S(2)}) %collective-permute-start.28) | collective-permute-done | bytes 163872 | tf_op jit(solution)/shard_map/ppermute | solution.py:412
  123.8 1.7 %collective-permute-start.31 = (bf16[208,128]{1,0:T(8,128)(2,1)S(1)}, bf16[208,128]{1,0:T(8,128)(2,1)S(1)}, u32[]{:S(2)}, u32[]{:S(2)}) collective-permute-start(bf16[208,128]{1,0:T(8,128)(2,1)S(1)} %get-tuple-element.92), channel_id=1, source_target_pairs={{0,64},{1,65},{2,66},{3,67},{4,68},{5,69},{6,70},{7,71},{8,72},{9,... | collective-permute-start | bytes 159752 | tf_op jit(solution)/shard_map/ppermute | solution.py:412
  125.5 2.1 %collective-permute-done.33.refs_2_ = bf16[208,128]{1,0:T(8,128)(2,1)S(1)} collective-permute-done((bf16[208,128]{1,0:T(8,128)(2,1)S(1)}, bf16[208,128]{1,0:T(8,128)(2,1)S(1)}, u32[]{:S(2)}, u32[]{:S(2)}) %collective-permute-start.33) | collective-permute-done | bytes 53280 | tf_op jit(solution)/shard_map/ppermute | solution.py:412
  127.6 1.7 %collective-permute-done.32.refs_1_ = bf16[208,128]{1,0:T(8,128)(2,1)S(1)} collective-permute-done((bf16[208,128]{1,0:T(8,128)(2,1)S(1)}, bf16[208,128]{1,0:T(8,128)(2,1)S(1)}, u32[]{:S(2)}, u32[]{:S(2)}) %collective-permute-start.32) | collective-permute-done | bytes 53280 | tf_op jit(solution)/shard_map/ppermute | solution.py:412
  129.3 1.0 collective-permute-done.31.refs_0_
  130.3 0.8 y_sum.1
  (81 shorter events, 5.9 us)
Async XLA Ops:
  2.3 3.8 %copy-start.4 = (f32[8,256]{1,0:T(8,128)S(1)}, f32[8,256]{1,0:T(8,128)}, u32[]{:S(2)}) copy-start(f32[8,256]{1,0:T(8,128)} %param.17) | copy-start | bytes 24580
  2.3 4.2 %copy-start.5 = (f32[8]{0:T(128)S(1)}, f32[8]{0:T(128)}, u32[]{:S(2)}) copy-start(f32[8]{0:T(128)} %param.16) | copy-start | bytes 100
  2.3 4.2 %copy-start.6 = (f32[8]{0:T(128)S(1)}, f32[8]{0:T(128)}, u32[]{:S(2)}) copy-start(f32[8]{0:T(128)} %param.15) | copy-start | bytes 100
  5.7 23.9 %copy-start.1 = (bf16[128,2048]{1,0:T(8,128)(2,1)S(1)}, bf16[128,2048]{1,0:T(8,128)(2,1)}, u32[]{:S(2)}) copy-start(bf16[128,2048]{1,0:T(8,128)(2,1)} %refs_8_) | copy-start | bytes 1572868
  6.8 7.4 %collective-permute-start.2 = (bf16[128,384]{1,0:T(8,128)(2,1)S(1)}, bf16[128,384]{1,0:T(8,128)(2,1)S(1)}, u32[]{:S(2)}, u32[]{:S(2)}) collective-permute-start(bf16[128,384]{1,0:T(8,128)(2,1)S(1)} %concatenate.27), channel_id=1, source_target_pairs={{0,65},{1,64},{2,67},{3,66},{4,69},{5,68},{6,71},{7,70},{8,73},{9,... | collective-permute-start | bytes 294920 | tf_op jit(solution)/shard_map/ppermute | solution.py:412
  10.0 6.8 %collective-permute-start.1 = (bf16[128,384]{1,0:T(8,128)(2,1)S(1)}, bf16[128,384]{1,0:T(8,128)(2,1)S(1)}, u32[]{:S(2)}, u32[]{:S(2)}) collective-permute-start(bf16[128,384]{1,0:T(8,128)(2,1)S(1)} %concatenate.27), channel_id=1, source_target_pairs={{0,1},{1,0},{2,3},{3,2},{4,5},{5,4},{6,7},{7,6},{8,9},{9,8},{10,11... | collective-permute-start | bytes 294920 | tf_op jit(solution)/shard_map/ppermute | solution.py:412
  10.7 7.2 %collective-permute-start = (bf16[128,384]{1,0:T(8,128)(2,1)S(1)}, bf16[128,384]{1,0:T(8,128)(2,1)S(1)}, u32[]{:S(2)}, u32[]{:S(2)}) collective-permute-start(bf16[128,384]{1,0:T(8,128)(2,1)S(1)} %concatenate.27), channel_id=1, source_target_pairs={{0,64},{1,65},{2,66},{3,67},{4,68},{5,69},{6,70},{7,71},{8,72},{9,... | collective-permute-start | bytes 294920 | tf_op jit(solution)/shard_map/ppermute | solution.py:412
  18.0 8.9 %collective-permute-start.5 = (bf16[128,384]{1,0:T(8,128)(2,1)S(1)}, bf16[128,384]{1,0:T(8,128)(2,1)S(1)}, u32[]{:S(2)}, u32[]{:S(2)}) collective-permute-start(bf16[128,384]{1,0:T(8,128)(2,1)S(1)} %concatenate.29), channel_id=1, source_target_pairs={{0,6},{1,7},{2,0},{3,1},{4,2},{5,3},{6,4},{7,5},{8,14},{9,15},{10,... | collective-permute-start | bytes 294920 | tf_op jit(solution)/shard_map/ppermute | solution.py:412
  22.1 6.6 %collective-permute-start.4 = (bf16[128,384]{1,0:T(8,128)(2,1)S(1)}, bf16[128,384]{1,0:T(8,128)(2,1)S(1)}, u32[]{:S(2)}, u32[]{:S(2)}) collective-permute-start(bf16[128,384]{1,0:T(8,128)(2,1)S(1)} %concatenate.29), channel_id=1, source_target_pairs={{0,4},{1,5},{2,6},{3,7},{4,0},{5,1},{6,2},{7,3},{8,12},{9,13},{10,... | collective-permute-start | bytes 294920 | tf_op jit(solution)/shard_map/ppermute | solution.py:412
  22.1 7.3 %collective-permute-start.3 = (bf16[128,384]{1,0:T(8,128)(2,1)S(1)}, bf16[128,384]{1,0:T(8,128)(2,1)S(1)}, u32[]{:S(2)}, u32[]{:S(2)}) collective-permute-start(bf16[128,384]{1,0:T(8,128)(2,1)S(1)} %concatenate.29), channel_id=1, source_target_pairs={{0,2},{1,3},{2,4},{3,5},{4,6},{5,7},{6,0},{7,1},{8,10},{9,11},{10,... | collective-permute-start | bytes 294920 | tf_op jit(solution)/shard_map/ppermute | solution.py:412
  23.3 18.5 %collective-permute-start.12 = (bf16[512,384]{1,0:T(8,128)(2,1)S(1)}, bf16[512,384]{1,0:T(8,128)(2,1)S(1)}, u32[]{:S(2)}, u32[]{:S(2)}) collective-permute-start(bf16[512,384]{1,0:T(8,128)(2,1)S(1)} %pad_maximum_fusion.1.col_ref), channel_id=1, source_target_pairs={{0,48},{1,49},{2,50},{3,51},{4,52},{5,53},{6,54},{7,55},{8,56},{9,... | collective-permute-start | bytes 1179656 | tf_op jit(solution)/shard_map/ppermute | solution.py:412
  26.1 18.3 %collective-permute-start.11 = (bf16[512,384]{1,0:T(8,128)(2,1)S(1)}, bf16[512,384]{1,0:T(8,128)(2,1)S(1)}, u32[]{:S(2)}, u32[]{:S(2)}) collective-permute-start(bf16[512,384]{1,0:T(8,128)(2,1)S(1)} %pad_maximum_fusion.1.col_ref), channel_id=1, source_target_pairs={{0,32},{1,33},{2,34},{3,35},{4,36},{5,37},{6,38},{7,39},{8,40},{9,... | collective-permute-start | bytes 1179656 | tf_op jit(solution)/shard_map/ppermute | solution.py:412
  26.9 18.6 %collective-permute-start.10 = (bf16[512,384]{1,0:T(8,128)(2,1)S(1)}, bf16[512,384]{1,0:T(8,128)(2,1)S(1)}, u32[]{:S(2)}, u32[]{:S(2)}) collective-permute-start(bf16[512,384]{1,0:T(8,128)(2,1)S(1)} %pad_maximum_fusion.1.col_ref), channel_id=1, source_target_pairs={{0,16},{1,17},{2,18},{3,19},{4,20},{5,21},{6,22},{7,23},{8,24},{9,... | collective-permute-start | bytes 1179656 | tf_op jit(solution)/shard_map/ppermute | solution.py:412
  27.8 17.9 %copy-start.2 = (bf16[256,128]{1,0:T(8,128)(2,1)S(1)}, bf16[256,128]{1,0:T(8,128)(2,1)}, u32[]{:S(2)}) copy-start(bf16[256,128]{1,0:T(8,128)(2,1)} %constant.91.clone.sel_ref) | copy-start | bytes 196612
  29.4 16.2 %collective-permute-start.9 = (bf16[512,384]{1,0:T(8,128)(2,1)S(1)}, bf16[512,384]{1,0:T(8,128)(2,1)S(1)}, u32[]{:S(2)}, u32[]{:S(2)}) collective-permute-start(bf16[512,384]{1,0:T(8,128)(2,1)S(1)} %pad_maximum_fusion.2), channel_id=1, source_target_pairs={{0,8},{1,9},{2,10},{3,11},{4,12},{5,13},{6,14},{7,15},{8,0},{9,1},... | collective-permute-start | bytes 1179656 | tf_op jit(solution)/shard_map/ppermute | solution.py:412
  29.7 51.2 %collective-permute-start.8 = (bf16[128,2048]{1,0:T(8,128)(2,1)S(1)}, bf16[128,2048]{1,0:T(8,128)(2,1)S(1)}, u32[]{:S(2)}, u32[]{:S(2)}) collective-permute-start(bf16[128,2048]{1,0:T(8,128)(2,1)S(1)} %copy-done.1), channel_id=1, source_target_pairs={{0,6},{1,7},{2,0},{3,1},{4,2},{5,3},{6,4},{7,5},{8,14},{9,15},{10,... | collective-permute-start | bytes 1572872 | tf_op jit(solution)/shard_map/ppermute | solution.py:412
  41.8 39.0 %collective-permute-start.7 = (bf16[128,2048]{1,0:T(8,128)(2,1)S(1)}, bf16[128,2048]{1,0:T(8,128)(2,1)S(1)}, u32[]{:S(2)}, u32[]{:S(2)}) collective-permute-start(bf16[128,2048]{1,0:T(8,128)(2,1)S(1)} %copy-done.1), channel_id=1, source_target_pairs={{0,4},{1,5},{2,6},{3,7},{4,0},{5,1},{6,2},{7,3},{8,12},{9,13},{10,... | collective-permute-start | bytes 1572872 | tf_op jit(solution)/shard_map/ppermute | solution.py:412
  44.4 36.4 %collective-permute-start.6 = (bf16[128,2048]{1,0:T(8,128)(2,1)S(1)}, bf16[128,2048]{1,0:T(8,128)(2,1)S(1)}, u32[]{:S(2)}, u32[]{:S(2)}) collective-permute-start(bf16[128,2048]{1,0:T(8,128)(2,1)S(1)} %copy-done.1), channel_id=1, source_target_pairs={{0,2},{1,3},{2,4},{3,5},{4,6},{5,7},{6,0},{7,1},{8,10},{9,11},{10,... | collective-permute-start | bytes 1572872 | tf_op jit(solution)/shard_map/ppermute | solution.py:412
  55.4 30.0 %copy-start.3 = (bf16[2048,1024]{1,0:T(8,128)(2,1)S(1)}, bf16[2048,1024]{1,0:T(8,128)(2,1)}, u32[]{:S(2)}) copy-start(bf16[2048,1024]{1,0:T(8,128)(2,1)} %param.11) | copy-start | bytes 12582916
  80.9 2.0 %collective-permute-start.13 = (f32[512,256]{1,0:T(8,128)S(1)}, f32[512,256]{1,0:T(8,128)S(1)}, u32[]{:S(2)}, u32[]{:S(2)}) collective-permute-start(f32[512,256]{1,0:T(8,128)S(1)} %slice.46), channel_id=1, source_target_pairs={{0,8},{1,9},{2,10},{3,11},{4,12},{5,13},{6,14},{7,15},{8,0},{9,1},... | collective-permute-start | bytes 1572872 | tf_op jit(solution)/shard_map/ppermute | solution.py:412
  81.2 16.4 %collective-permute-start.20 = (bf16[128,2048]{1,0:T(8,128)(2,1)S(1)}, bf16[128,2048]{1,0:T(8,128)(2,1)S(1)}, u32[]{:S(2)}, u32[]{:S(2)}) collective-permute-start(bf16[128,2048]{1,0:T(8,128)(2,1)S(1)} %copy-done.1), channel_id=1, source_target_pairs={{0,8},{1,9},{2,10},{3,11},{4,12},{5,13},{6,14},{7,15},{8,0},{9,1},... | collective-permute-start | bytes 1572872 | tf_op jit(solution)/shard_map/ppermute | solution.py:412
  81.7 16.7 %collective-permute-start.21 = (bf16[128,2048]{1,0:T(8,128)(2,1)S(1)}, bf16[128,2048]{1,0:T(8,128)(2,1)S(1)}, u32[]{:S(2)}, u32[]{:S(2)}) collective-permute-start(bf16[128,2048]{1,0:T(8,128)(2,1)S(1)} %collective-permute-done.6.refs_1_.refs_9_), channel_id=1, source_target_pairs={{0,8},{1,9},{2,10},{3,11},{4,12},{5,13},{6,14},{7,15},{8,0},{9,1},... | collective-permute-start | bytes 1572872 | tf_op jit(solution)/shard_map/ppermute | solution.py:412
  81.8 17.9 %collective-permute-start.22 = (bf16[128,2048]{1,0:T(8,128)(2,1)S(1)}, bf16[128,2048]{1,0:T(8,128)(2,1)S(1)}, u32[]{:S(2)}, u32[]{:S(2)}) collective-permute-start(bf16[128,2048]{1,0:T(8,128)(2,1)S(1)} %collective-permute-done.7.refs_2_.refs_10_), channel_id=1, source_target_pairs={{0,8},{1,9},{2,10},{3,11},{4,12},{5,13},{6,14},{7,15},{8,0},{9,1},... | collective-permute-start | bytes 1572872 | tf_op jit(solution)/shard_map/ppermute | solution.py:412
  83.0 4.7 %collective-permute-start.14 = (bf16[128,256]{1,0:T(8,128)(2,1)S(1)}, bf16[128,256]{1,0:T(8,128)(2,1)S(1)}, u32[]{:S(2)}, u32[]{:S(2)}) collective-permute-start(bf16[128,256]{1,0:T(8,128)(2,1)S(1)} %get-tuple-element.87), channel_id=1, source_target_pairs={{0,6},{1,7},{2,0},{3,1},{4,2},{5,3},{6,4},{7,5},{8,14},{9,15},{10,... | collective-permute-start | bytes 196616 | tf_op jit(solution)/shard_map/ppermute | solution.py:412
  85.4 5.5 %collective-permute-start.16 = (bf16[128,256]{1,0:T(8,128)(2,1)S(1)}, bf16[128,256]{1,0:T(8,128)(2,1)S(1)}, u32[]{:S(2)}, u32[]{:S(2)}) collective-permute-start(bf16[128,256]{1,0:T(8,128)(2,1)S(1)} %get-tuple-element.88), channel_id=1, source_target_pairs={{0,2},{1,3},{2,4},{3,5},{4,6},{5,7},{6,0},{7,1},{8,10},{9,11},{10,... | collective-permute-start | bytes 196616 | tf_op jit(solution)/shard_map/ppermute | solution.py:412
  87.7 12.0 %collective-permute-start.23 = (bf16[128,2048]{1,0:T(8,128)(2,1)S(1)}, bf16[128,2048]{1,0:T(8,128)(2,1)S(1)}, u32[]{:S(2)}, u32[]{:S(2)}) collective-permute-start(bf16[128,2048]{1,0:T(8,128)(2,1)S(1)} %collective-permute-done.8.refs_3_.refs_11_), channel_id=1, source_target_pairs={{0,8},{1,9},{2,10},{3,11},{4,12},{5,13},{6,14},{7,15},{8,0},{9,1},... | collective-permute-start | bytes 1572872 | tf_op jit(solution)/shard_map/ppermute | solution.py:412
  90.8 5.8 %collective-permute-start.15 = (bf16[128,256]{1,0:T(8,128)(2,1)S(1)}, bf16[128,256]{1,0:T(8,128)(2,1)S(1)}, u32[]{:S(2)}, u32[]{:S(2)}) collective-permute-start(bf16[128,256]{1,0:T(8,128)(2,1)S(1)} %get-tuple-element.89), channel_id=1, source_target_pairs={{0,4},{1,5},{2,6},{3,7},{4,0},{5,1},{6,2},{7,3},{8,12},{9,13},{10,... | collective-permute-start | bytes 196616 | tf_op jit(solution)/shard_map/ppermute | solution.py:412
  97.3 9.2 %copy-start = (bf16[1024,256]{1,0:T(8,128)(2,1)S(1)}, bf16[1024,256]{1,0:T(8,128)(2,1)}, u32[]{:S(2)}) copy-start(bf16[1024,256]{1,0:T(8,128)(2,1)} %w_ref.1) | copy-start | bytes 1572868
  97.3 4.9 %collective-permute-start.19 = (bf16[160,256]{1,0:T(8,128)(2,1)S(1)}, bf16[160,256]{1,0:T(8,128)(2,1)S(1)}, u32[]{:S(2)}, u32[]{:S(2)}) collective-permute-start(bf16[160,256]{1,0:T(8,128)(2,1)S(1)} %pad_maximum_fusion.3.refs_0_), channel_id=1, source_target_pairs={{0,6},{1,7},{2,0},{3,1},{4,2},{5,3},{6,4},{7,5},{8,14},{9,15},{10,... | collective-permute-start | bytes 245768 | tf_op jit(solution)/shard_map/ppermute | solution.py:412
  97.6 6.1 %collective-permute-start.18 = (bf16[160,256]{1,0:T(8,128)(2,1)S(1)}, bf16[160,256]{1,0:T(8,128)(2,1)S(1)}, u32[]{:S(2)}, u32[]{:S(2)}) collective-permute-start(bf16[160,256]{1,0:T(8,128)(2,1)S(1)} %pad_maximum_fusion.3.refs_0_), channel_id=1, source_target_pairs={{0,4},{1,5},{2,6},{3,7},{4,0},{5,1},{6,2},{7,3},{8,12},{9,13},{10,... | collective-permute-start | bytes 245768 | tf_op jit(solution)/shard_map/ppermute | solution.py:412
  98.5 6.2 %collective-permute-start.17 = (bf16[160,256]{1,0:T(8,128)(2,1)S(1)}, bf16[160,256]{1,0:T(8,128)(2,1)S(1)}, u32[]{:S(2)}, u32[]{:S(2)}) collective-permute-start(bf16[160,256]{1,0:T(8,128)(2,1)S(1)} %pad_maximum_fusion.3.refs_0_), channel_id=1, source_target_pairs={{0,2},{1,3},{2,4},{3,5},{4,6},{5,7},{6,0},{7,1},{8,10},{9,11},{10,... | collective-permute-start | bytes 245768 | tf_op jit(solution)/shard_map/ppermute | solution.py:412
  104.6 1.3 collective-permute-start.24
  104.6 1.4 %collective-permute-start.25 = (bf16[160,256]{1,0:T(8,128)(2,1)S(1)}, bf16[160,256]{1,0:T(8,128)(2,1)S(1)}, u32[]{:S(2)}, u32[]{:S(2)}) collective-permute-start(bf16[160,256]{1,0:T(8,128)(2,1)S(1)} %collective-permute-done.17.refs_1_), channel_id=1, source_target_pairs={{0,8},{1,9},{2,10},{3,11},{4,12},{5,13},{6,14},{7,15},{8,0},{9,1},... | collective-permute-start | bytes 245768 | tf_op jit(solution)/shard_map/ppermute | solution.py:412
  105.1 1.3 collective-permute-start.26
  105.1 1.4 %collective-permute-start.27 = (bf16[160,256]{1,0:T(8,128)(2,1)S(1)}, bf16[160,256]{1,0:T(8,128)(2,1)S(1)}, u32[]{:S(2)}, u32[]{:S(2)}) collective-permute-start(bf16[160,256]{1,0:T(8,128)(2,1)S(1)} %collective-permute-done.19.refs_3_), channel_id=1, source_target_pairs={{0,8},{1,9},{2,10},{3,11},{4,12},{5,13},{6,14},{7,15},{8,0},{9,1},... | collective-permute-start | bytes 245768 | tf_op jit(solution)/shard_map/ppermute | solution.py:412
  108.8 11.1 %collective-permute-start.30 = (bf16[640,128]{1,0:T(8,128)(2,1)S(1)}, bf16[640,128]{1,0:T(8,128)(2,1)S(1)}, u32[]{:S(2)}, u32[]{:S(2)}) collective-permute-start(bf16[640,128]{1,0:T(8,128)(2,1)S(1)} %get-tuple-element.84), channel_id=1, source_target_pairs={{0,48},{1,49},{2,50},{3,51},{4,52},{5,53},{6,54},{7,55},{8,56},{9,... | collective-permute-start | bytes 491528 | tf_op jit(solution)/shard_map/ppermute | solution.py:412
  112.4 8.6 %collective-permute-start.29 = (bf16[640,128]{1,0:T(8,128)(2,1)S(1)}, bf16[640,128]{1,0:T(8,128)(2,1)S(1)}, u32[]{:S(2)}, u32[]{:S(2)}) collective-permute-start(bf16[640,128]{1,0:T(8,128)(2,1)S(1)} %get-tuple-element.85), channel_id=1, source_target_pairs={{0,32},{1,33},{2,34},{3,35},{4,36},{5,37},{6,38},{7,39},{8,40},{9,... | collective-permute-start | bytes 491528 | tf_op jit(solution)/shard_map/ppermute | solution.py:412
  112.4 10.9 %collective-permute-start.28 = (bf16[640,128]{1,0:T(8,128)(2,1)S(1)}, bf16[640,128]{1,0:T(8,128)(2,1)S(1)}, u32[]{:S(2)}, u32[]{:S(2)}) collective-permute-start(bf16[640,128]{1,0:T(8,128)(2,1)S(1)} %get-tuple-element.86), channel_id=1, source_target_pairs={{0,16},{1,17},{2,18},{3,19},{4,20},{5,21},{6,22},{7,23},{8,24},{9,... | collective-permute-start | bytes 491528 | tf_op jit(solution)/shard_map/ppermute | solution.py:412
  123.4 4.2 %collective-permute-start.33 = (bf16[208,128]{1,0:T(8,128)(2,1)S(1)}, bf16[208,128]{1,0:T(8,128)(2,1)S(1)}, u32[]{:S(2)}, u32[]{:S(2)}) collective-permute-start(bf16[208,128]{1,0:T(8,128)(2,1)S(1)} %get-tuple-element.90), channel_id=1, source_target_pairs={{0,65},{1,64},{2,67},{3,66},{4,69},{5,68},{6,71},{7,70},{8,73},{9,... | collective-permute-start | bytes 159752 | tf_op jit(solution)/shard_map/ppermute | solution.py:412
  123.5 5.8 %collective-permute-start.32 = (bf16[208,128]{1,0:T(8,128)(2,1)S(1)}, bf16[208,128]{1,0:T(8,128)(2,1)S(1)}, u32[]{:S(2)}, u32[]{:S(2)}) collective-permute-start(bf16[208,128]{1,0:T(8,128)(2,1)S(1)} %get-tuple-element.91), channel_id=1, source_target_pairs={{0,1},{1,0},{2,3},{3,2},{4,5},{5,4},{6,7},{7,6},{8,9},{9,8},{10,11... | collective-permute-start | bytes 159752 | tf_op jit(solution)/shard_map/ppermute | solution.py:412
  123.8 6.5 %collective-permute-start.31 = (bf16[208,128]{1,0:T(8,128)(2,1)S(1)}, bf16[208,128]{1,0:T(8,128)(2,1)S(1)}, u32[]{:S(2)}, u32[]{:S(2)}) collective-permute-start(bf16[208,128]{1,0:T(8,128)(2,1)S(1)} %get-tuple-element.92), channel_id=1, source_target_pairs={{0,64},{1,65},{2,66},{3,67},{4,68},{5,69},{6,70},{7,71},{8,72},{9,... | collective-permute-start | bytes 159752 | tf_op jit(solution)/shard_map/ppermute | solution.py:412
